TPU v7x, 512 devices: a whole 4x8x8 slice. The times are simulated.
512 devices in a mesh: grp: 8 (over x, core), dev: 64 (over z, y).
Axes of the slice: x: 4, y: 8, z: 8, core: 2. Of those that a mesh axis runs over, the one named last changes fastest.
Arguments:
- diag_inverse: bfloat16 [1024, 512, 512], P(('grp', 'dev')), may hold values from -1 to 1.5, as said below
- lower_block: bfloat16 [1024, 512, 512], P(('grp', 'dev')), may hold values from -0.15625 to 0.15625
- upper_block: bfloat16 [1024, 512, 512], P(('grp', 'dev')), may hold values from -0.15625 to 0.15625
- right_side: bfloat16 [1024, 512, 128], P(('grp', 'dev')), may hold values from -6 to 6
Outputs:
- solution: bfloat16 [1024, 512, 128], P(('grp', 'dev'))
Inputs may be any that keep to these rules, and one draw needn't show every extreme that they name: diag_inverse holds the given inverses of the diagonal blocks.
All inputs are finite; a program needn't handle non-finite values.
Results may differ from a plain program's by a relative error of at most 0.013.
Values may be sent and summed in bfloat16 or wider, within the bound.
A program may use at most 64 MiB of HBM per device.

v0:
```python
import jax
import jax.numpy as jnp
from jax import lax
from jax.sharding import PartitionSpec as P


def passed_along(block, axis, distance):
    devices = range(lax.axis_size(axis))
    route = [(i - distance, i) for i in devices if i - distance in devices]
    return lax.ppermute(block, axis, route)


def reduce_panel(middle, left_panel, right_panel, order):
    left_spike = middle[:, :order]
    right_spike = middle[:, order : 2 * order]
    own_rhs = middle[:, 2 * order :]
    from_left = jnp.dot(left_spike, left_panel, preferred_element_type=jnp.float32)
    from_right = jnp.dot(right_spike, right_panel, preferred_element_type=jnp.float32)
    coupling = from_left[:, order : 2 * order] + from_right[:, :order]
    scaling = (jnp.eye(order, dtype=jnp.float32) + coupling).astype(jnp.bfloat16)
    outer_left = from_left[:, :order].astype(jnp.bfloat16)
    outer_right = from_right[:, order : 2 * order].astype(jnp.bfloat16)
    remaining = (
        own_rhs.astype(jnp.float32) - from_left[:, 2 * order :] - from_right[:, 2 * order :]
    ).astype(jnp.bfloat16)
    combined = jnp.concatenate([-outer_left, -outer_right, remaining], axis=1)
    return jnp.dot(scaling, combined, preferred_element_type=jnp.float32).astype(jnp.bfloat16)


def apply_panel(middle, left_values, right_values, order):
    left_spike = middle[:, :order]
    right_spike = middle[:, order : 2 * order]
    own_rhs = middle[:, 2 * order :].astype(jnp.float32)
    total = own_rhs - jnp.dot(left_spike, left_values, preferred_element_type=jnp.float32)
    total = total - jnp.dot(right_spike, right_values, preferred_element_type=jnp.float32)
    return total.astype(jnp.bfloat16)


def make_panels(diag_inverse, lower_block, upper_block, right_side):
    rows_made = []
    for row in range(diag_inverse.shape[0]):
        stacked = jnp.concatenate([lower_block[row], upper_block[row], right_side[row]], axis=1)
        rows_made.append(
            jnp.dot(diag_inverse[row], stacked, preferred_element_type=jnp.float32).astype(
                jnp.bfloat16
            )
        )
    return jnp.stack(rows_made)


def body(diag_inverse, lower_block, upper_block, right_side):
    order = diag_inverse.shape[1]
    own_panels = make_panels(diag_inverse, lower_block, upper_block, right_side)
    before = passed_along(own_panels[1], ("grp", "dev"), 1)
    level_one = reduce_panel(own_panels[0], before, own_panels[1], order)
    beside = [passed_along(level_one, ("grp", "dev"), offset) for offset in (1, -1)]
    level_two = reduce_panel(level_one, beside[0], beside[1], order)
    coarse = level_two[:, 2 * order :]
    coarse_side = [passed_along(coarse, ("grp", "dev"), offset) for offset in (2, -2)]
    even_values = apply_panel(level_two, coarse_side[0], coarse_side[1], order)
    next_even = passed_along(even_values, ("grp", "dev"), -1)
    odd_values = apply_panel(own_panels[1], even_values, next_even, order)
    return jnp.stack([even_values, odd_values])


def solution(mesh):
    return jax.shard_map(
        body,
        mesh=mesh,
        in_specs=(
            P(("grp", "dev"), None, None),
            P(("grp", "dev"), None, None),
            P(("grp", "dev"), None, None),
            P(("grp", "dev"), None, None),
        ),
        out_specs=P(("grp", "dev"), None, None),
        check_vma=False,
    )
```

profile of v0, /device:TPU:6, one launch (start us, length us, event | category | flops | bytes accessed | tf_op | source)
XLA Modules:
  0.0 117.7 jit_solution(4940070656790698133)
XLA Ops:
  0.0 1.0 slice_bitcast_fusion.5
  1.0 0.0 copy-start.2
  1.0 1.7 %slice_bitcast_fusion.2 = (bf16[512,512]{1,0:T(8,128)(2,1)S(1)}, bf16[512,512]{1,0:T(8,128)(2,1)S(1)}, bf16[512,512]{1,0:T(8,128)(2,1)S(1)}, bf16[512,512]{1,0:T(8,128)(2,1)S(1)}) fusion(bf16[2,512,512]{2,1,0:T(8,128)(2,1)} %param.6, bf16[2,512,512]{2,1,0:T(8,128)(2,1)} %param.5), kind=kLoop, calls=%fused_computation.66 | loop fusion | bytes 4194304 | tf_op jit(solution)/shard_map/squeeze | solution.py:42
  2.7 0.1 copy-done.2
  2.8 0.8 convolution_convert_fusion.2
  3.7 3.5 %collective-permute-start = (bf16[512,1152]{0,1:T(8,128)(2,1)S(1)}, bf16[512,1152]{0,1:T(8,128)(2,1)}, u32[]{:S(2)}, u32[]{:S(2)}) collective-permute-start(bf16[512,1152]{0,1:T(8,128)(2,1)S(1)} %bitcast.32), channel_id=1, source_target_pairs={{0,1},{1,2},{2,3},{3,4},{4,5},{5,6},{6,7},{7,8},{8,9},{9,10},{10,1... | collective-permute-start | bytes 3538952 | tf_op jit(solution)/shard_map/ppermute | solution.py:10
  7.2 0.8 fusion
  8.0 0.0 copy-start.1
  8.0 0.9 fusion.42
  8.9 0.1 copy-done.1
  9.1 0.7 slice.141
  9.8 1.8 %copy.20 = f32[512,128]{0,1:T(8,128)} copy(f32[512,128]{1,0:T(8,128)} %slice.141) | data formatting | bytes 524288
  11.5 0.9 fusion.28
  12.4 30.6 %collective-permute-done = bf16[512,1152]{0,1:T(8,128)(2,1)} collective-permute-done((bf16[512,1152]{0,1:T(8,128)(2,1)S(1)}, bf16[512,1152]{0,1:T(8,128)(2,1)}, u32[]{:S(2)}, u32[]{:S(2)}) %collective-permute-start) | collective-permute-done | bytes 1179680 | tf_op jit(solution)/shard_map/ppermute | solution.py:10
  43.0 2.3 %fusion.44 = f32[512,1152]{1,0:T(8,128)S(1)} fusion(bf16[512,1152]{0,1:T(8,128)(2,1)} %collective-permute-done, bf16[512,1152]{0,1:T(8,128)(2,1)} %copy-done.1), kind=kOutput, calls=%fused_computation.58 | convolution fusion | flops 603979776 | bytes 4063232 | tf_op jit(solution)/shard_map/dot_general | solution.py:17
  45.3 0.0 copy-start
  45.3 0.8 slice.140
  46.1 0.7 copy-done
  46.8 0.8 fusion.27
  47.7 1.8 %copy.19 = f32[512,128]{0,1:T(8,128)} copy(f32[512,128]{1,0:T(8,128)} %slice.140) | data formatting | bytes 524288
  49.4 1.8 %subtract_convert_fusion = bf16[512,128]{0,1:T(8,128)(2,1)} fusion(f32[512,128]{0,1:T(8,128)} %copy.20, f32[512,128]{0,1:T(8,128)} %copy.19, bf16[512,1152]{0,1:T(8,128)(2,1)} %copy-done.1), kind=kLoop, calls=%fused_computation.72 | loop fusion | flops 262144 | bytes 786432 | tf_op jit(solution)/shard_map/convert_element_type | solution.py:25
  51.2 1.7 %copy.7 = bf16[512,128]{1,0:T(8,128)(2,1)} copy(bf16[512,128]{0,1:T(8,128)(2,1)} %subtract_convert_fusion) | data formatting | bytes 262144 | tf_op jit(solution)/shard_map/convert_element_type | solution.py:25
  52.9 2.4 %convolution_convert_fusion.1 = bf16[512,1152]{1,0:T(8,128)(2,1)S(1)} fusion(bf16[512,128]{1,0:T(8,128)(2,1)} %copy.7, bf16[512,512]{1,0:T(8,128)(2,1)} %fusion.28, bf16[512,512]{1,0:T(8,128)(2,1)} %fusion.27, f32[512,1152]{1,0:T(8,128)S(1)} %fusion.42, f32[512,1152]{1,0:T(8,128)} %copy-done), kind=kOutput, calls=%fused_computation.1 | convolution fusion | flops 609419264 | bytes 4456448 | tf_op jit(solution)/shard_map/dot_general | solution.py:27
  55.3 3.1 %collective-permute-start.2 = (bf16[512,1152]{1,0:T(8,128)(2,1)S(1)}, bf16[512,1152]{1,0:T(8,128)(2,1)S(1)}, u32[]{:S(2)}, u32[]{:S(2)}) collective-permute-start(bf16[512,1152]{1,0:T(8,128)(2,1)S(1)} %convolution_convert_fusion.1), channel_id=1, source_target_pairs={{1,0},{2,1},{3,2},{4,3},{5,4},{6,5},{7,6},{8,7},{9,8},{10,9},{11,1... | collective-permute-start | bytes 3538952 | tf_op jit(solution)/shard_map/ppermute | solution.py:10
  58.4 2.8 %collective-permute-start.1 = (bf16[512,1152]{1,0:T(8,128)(2,1)S(1)}, bf16[512,1152]{1,0:T(8,128)(2,1)S(1)}, u32[]{:S(2)}, u32[]{:S(2)}) collective-permute-start(bf16[512,1152]{1,0:T(8,128)(2,1)S(1)} %convolution_convert_fusion.1), channel_id=1, source_target_pairs={{0,1},{1,2},{2,3},{3,4},{4,5},{5,6},{6,7},{7,8},{8,9},{9,10},{10,1... | collective-permute-start | bytes 3538952 | tf_op jit(solution)/shard_map/ppermute | solution.py:10
  61.1 23.0 %collective-permute-done.2 = bf16[512,1152]{1,0:T(8,128)(2,1)S(1)} collective-permute-done((bf16[512,1152]{1,0:T(8,128)(2,1)S(1)}, bf16[512,1152]{1,0:T(8,128)(2,1)S(1)}, u32[]{:S(2)}, u32[]{:S(2)}) %collective-permute-start.2) | collective-permute-done | bytes 1179680 | tf_op jit(solution)/shard_map/ppermute | solution.py:10
  84.1 0.8 fusion.38
  85.0 0.1 fusion.30
  85.0 6.9 %collective-permute-done.1 = bf16[512,1152]{1,0:T(8,128)(2,1)S(1)} collective-permute-done((bf16[512,1152]{1,0:T(8,128)(2,1)S(1)}, bf16[512,1152]{1,0:T(8,128)(2,1)S(1)}, u32[]{:S(2)}, u32[]{:S(2)}) %collective-permute-start.1) | collective-permute-done | bytes 1179680 | tf_op jit(solution)/shard_map/ppermute | solution.py:10
  91.9 0.8 fusion.40
  92.8 0.1 fusion.29
  92.9 0.8 convolution_convert_fusion
  93.7 1.9 %collective-permute-start.4 = (bf16[512,128]{0,1:T(8,128)(2,1)S(1)}, bf16[512,128]{0,1:T(8,128)(2,1)S(1)}, u32[]{:S(2)}, u32[]{:S(2)}) collective-permute-start(bf16[512,128]{0,1:T(8,128)(2,1)S(1)} %slice.151), channel_id=1, source_target_pairs={{2,0},{3,1},{4,2},{5,3},{6,4},{7,5},{8,6},{9,7},{10,8},{11,9},{12,... | collective-permute-start | bytes 393224 | tf_op jit(solution)/shard_map/ppermute | solution.py:10
  95.7 4.8 %collective-permute-start.3 = (bf16[512,128]{0,1:T(8,128)(2,1)S(1)}, bf16[512,128]{0,1:T(8,128)(2,1)S(1)}, u32[]{:S(2)}, u32[]{:S(2)}) collective-permute-start(bf16[512,128]{0,1:T(8,128)(2,1)S(1)} %slice.151), channel_id=1, source_target_pairs={{0,2},{1,3},{2,4},{3,5},{4,6},{5,7},{6,8},{7,9},{8,10},{9,11},{10,... | collective-permute-start | bytes 393224 | tf_op jit(solution)/shard_map/ppermute | solution.py:10
  100.5 1.1 collective-permute-done.4
  101.6 0.2 fusion.35
  101.8 6.7 %collective-permute-done.3 = bf16[512,128]{0,1:T(8,128)(2,1)S(1)} collective-permute-done((bf16[512,128]{0,1:T(8,128)(2,1)S(1)}, bf16[512,128]{0,1:T(8,128)(2,1)S(1)}, u32[]{:S(2)}, u32[]{:S(2)}) %collective-permute-start.3) | collective-permute-done | bytes 131104 | tf_op jit(solution)/shard_map/ppermute | solution.py:10
  108.5 0.2 fusion.23
  108.7 2.7 %collective-permute-start.5 = (bf16[512,128]{0,1:T(8,128)(2,1)S(1)}, bf16[512,128]{0,1:T(8,128)(2,1)S(1)}, u32[]{:S(2)}, u32[]{:S(2)}) collective-permute-start(bf16[512,128]{0,1:T(8,128)(2,1)S(1)} %fusion.23), channel_id=1, source_target_pairs={{1,0},{2,1},{3,2},{4,3},{5,4},{6,5},{7,6},{8,7},{9,8},{10,9},{11,1... | collective-permute-start | bytes 393224 | tf_op jit(solution)/shard_map/ppermute | solution.py:10
  111.5 0.2 convolution_subtract_fusion.1
  111.7 4.9 %collective-permute-done.5 = bf16[512,128]{0,1:T(8,128)(2,1)S(1)} collective-permute-done((bf16[512,128]{0,1:T(8,128)(2,1)S(1)}, bf16[512,128]{0,1:T(8,128)(2,1)S(1)}, u32[]{:S(2)}, u32[]{:S(2)}) %collective-permute-start.5) | collective-permute-done | bytes 131104 | tf_op jit(solution)/shard_map/ppermute | solution.py:10
  116.6 0.2 fusion.24
  116.9 0.8 copy.13
  (3 shorter events, 0.1 us)
Async XLA Ops:
  1.0 1.9 %copy-start.2 = (bf16[2,512,512]{2,1,0:T(8,128)(2,1)S(1)}, bf16[2,512,512]{2,1,0:T(8,128)(2,1)}, u32[]{:S(2)}) copy-start(bf16[2,512,512]{2,1,0:T(8,128)(2,1)} %param.4) | copy-start | bytes 3145732
  3.7 39.3 %collective-permute-start = (bf16[512,1152]{0,1:T(8,128)(2,1)S(1)}, bf16[512,1152]{0,1:T(8,128)(2,1)}, u32[]{:S(2)}, u32[]{:S(2)}) collective-permute-start(bf16[512,1152]{0,1:T(8,128)(2,1)S(1)} %bitcast.32), channel_id=1, source_target_pairs={{0,1},{1,2},{2,3},{3,4},{4,5},{5,6},{6,7},{7,8},{8,9},{9,10},{10,1... | collective-permute-start | bytes 3538952 | tf_op jit(solution)/shard_map/ppermute | solution.py:10
  8.0 1.0 copy-start.1
  45.3 1.5 %copy-start = (f32[512,1152]{1,0:T(8,128)}, f32[512,1152]{1,0:T(8,128)S(1)}, u32[]{:S(2)}) copy-start(f32[512,1152]{1,0:T(8,128)S(1)} %fusion.44) | copy-start | bytes 7077892
  55.3 28.8 %collective-permute-start.2 = (bf16[512,1152]{1,0:T(8,128)(2,1)S(1)}, bf16[512,1152]{1,0:T(8,128)(2,1)S(1)}, u32[]{:S(2)}, u32[]{:S(2)}) collective-permute-start(bf16[512,1152]{1,0:T(8,128)(2,1)S(1)} %convolution_convert_fusion.1), channel_id=1, source_target_pairs={{1,0},{2,1},{3,2},{4,3},{5,4},{6,5},{7,6},{8,7},{9,8},{10,9},{11,1... | collective-permute-start | bytes 3538952 | tf_op jit(solution)/shard_map/ppermute | solution.py:10
  58.4 33.6 %collective-permute-start.1 = (bf16[512,1152]{1,0:T(8,128)(2,1)S(1)}, bf16[512,1152]{1,0:T(8,128)(2,1)S(1)}, u32[]{:S(2)}, u32[]{:S(2)}) collective-permute-start(bf16[512,1152]{1,0:T(8,128)(2,1)S(1)} %convolution_convert_fusion.1), channel_id=1, source_target_pairs={{0,1},{1,2},{2,3},{3,4},{4,5},{5,6},{6,7},{7,8},{8,9},{9,10},{10,1... | collective-permute-start | bytes 3538952 | tf_op jit(solution)/shard_map/ppermute | solution.py:10
  93.7 7.9 %collective-permute-start.4 = (bf16[512,128]{0,1:T(8,128)(2,1)S(1)}, bf16[512,128]{0,1:T(8,128)(2,1)S(1)}, u32[]{:S(2)}, u32[]{:S(2)}) collective-permute-start(bf16[512,128]{0,1:T(8,128)(2,1)S(1)} %slice.151), channel_id=1, source_target_pairs={{2,0},{3,1},{4,2},{5,3},{6,4},{7,5},{8,6},{9,7},{10,8},{11,9},{12,... | collective-permute-start | bytes 393224 | tf_op jit(solution)/shard_map/ppermute | solution.py:10
  95.7 12.8 %collective-permute-start.3 = (bf16[512,128]{0,1:T(8,128)(2,1)S(1)}, bf16[512,128]{0,1:T(8,128)(2,1)S(1)}, u32[]{:S(2)}, u32[]{:S(2)}) collective-permute-start(bf16[512,128]{0,1:T(8,128)(2,1)S(1)} %slice.151), channel_id=1, source_target_pairs={{0,2},{1,3},{2,4},{3,5},{4,6},{5,7},{6,8},{7,9},{8,10},{9,11},{10,... | collective-permute-start | bytes 393224 | tf_op jit(solution)/shard_map/ppermute | solution.py:10
  108.7 7.9 %collective-permute-start.5 = (bf16[512,128]{0,1:T(8,128)(2,1)S(1)}, bf16[512,128]{0,1:T(8,128)(2,1)S(1)}, u32[]{:S(2)}, u32[]{:S(2)}) collective-permute-start(bf16[512,128]{0,1:T(8,128)(2,1)S(1)} %fusion.23), channel_id=1, source_target_pairs={{1,0},{2,1},{3,2},{4,3},{5,4},{6,5},{7,6},{8,7},{9,8},{10,9},{11,1... | collective-permute-start | bytes 393224 | tf_op jit(solution)/shard_map/ppermute | solution.py:10
where the time goes:
time: 119 us; the launch traced here: 118 us
  waiting for transfers between devices  73.2 us (62%)
  starting transfers between devices  18.8 us (16%)
  local copies, waits for them, and re-layouts  11.2 us (9%)
  matrix products  10.7 us (9%)
  other arithmetic  3.64 us (3%)
    ppermute x6, waiting for transfers between devices, passed_along(): return lax.ppermute(block, axis, route)  73.2 us
    ppermute x6, starting transfers between devices, passed_along(): return lax.ppermute(block, axis, route)  18.8 us
    unnamed x8, local copies, waits for them, and re-layouts  4.51 us
    dot_general x2, matrix products, reduce_panel(): jnp.dot(scaling, combined, preferred_element_type=jnp.float32)  3.22 us
    dot_general x2, matrix products, reduce_panel(): jnp.dot(left_spike, left_panel, preferred_element_type=jnp.float32)  3.16 us
  transfers between devices with their start and end apart: 6, of which 6 were waited for; matrix products, arithmetic and copies ran while one was open for 5% of the time, Pallas kernels for 0%

commit v1 on v0

v1 whole, which is shorter than its diff:
```python
import jax
import jax.numpy as jnp
from jax import lax
from jax.experimental import pallas as pl
from jax.experimental.pallas import tpu as pltpu
from jax.sharding import PartitionSpec as P

F32, BF16 = jnp.float32, jnp.bfloat16
MESH = pl.DeviceIdType.MESH
ROWS = ((0, 256), (256, 128), (384, 128))
HALVES = ((0, 256), (256, 256))


def mm(a, b):
    return jnp.dot(a, b, preferred_element_type=F32)


def mv(rows, matrix):
    return lax.dot_general(rows, matrix, (((1,), (1,)), ((), ())), preferred_element_type=F32)


def sweep(groups, slab, diag, lower, upper, right, out, bufs, rhs, zl, zr, fsum, sent, zero, narrow, wide, load, tx, rx):
    n = diag.shape[1]
    total = groups * slab
    me = lax.axis_index("grp") * slab + lax.axis_index("dev")
    has_l, has_r = me > 0, me < total - 1
    at_l, at_r = lax.rem(me + total - 1, total), lax.rem(me + 1, total)
    left = (at_l // slab, lax.rem(at_l, slab))
    right_id = (at_r // slab, lax.rem(at_r, slab))
    (do, uo, lo, de, le, ue) = (bufs.at[i] for i in range(6))
    (A, B, C, E, J, K, CA, T, V, CV, EL, TL, CVL, WR, S, EA, EJ) = (
        bufs.at[i] for i in range(6, 23)
    )
    ro, re = rhs.at[0], rhs.at[1]

    barrier = pltpu.get_barrier_semaphore()

    @pl.when(has_l)
    def _():
        pl.semaphore_signal(barrier, 1, device_id=left, device_id_type=MESH)

    @pl.when(has_r)
    def _():
        pl.semaphore_signal(barrier, 1, device_id=right_id, device_id_type=MESH)

    loads = {}
    order = (
        ("do", diag.at[1], do), ("uo", upper.at[1], uo), ("ro", right.at[1], ro),
        ("lo", lower.at[1], lo), ("de", diag.at[0], de), ("ue", upper.at[0], ue),
        ("le", lower.at[0], le), ("re", right.at[0], re),
    )
    for i, (name, src, dst) in enumerate(order):
        loads[name] = pltpu.make_async_copy(src, dst, load.at[i])
        loads[name].start()

    moves = []

    class Move:
        def __init__(self, src, dst, rightward):
            i = len(moves)
            moves.append(self)
            self.dst, self.sem = dst, rx.at[i]
            self.to, self.come = (has_r, has_l) if rightward else (has_l, has_r)
            self.copy = pltpu.make_async_remote_copy(
                src_ref=src, dst_ref=dst, send_sem=tx.at[i], recv_sem=rx.at[i],
                device_id=right_id if rightward else left, device_id_type=MESH,
            )

        def start(self):
            pl.when(self.to)(self.copy.start)

        def blank(self):
            rows = self.dst.shape[0]
            self.zero = pltpu.make_async_copy(zero.at[pl.ds(0, rows)], self.dst, self.sem)
            pl.when(jnp.logical_not(self.come))(self.zero.start)

        def arrive(self):
            self.copy.wait_recv()

        def drain(self):
            pl.when(self.to)(self.copy.wait_send)

    zero[...] = jnp.zeros_like(zero)

    h, cg, m1, m2 = (sent.at[i] for i in range(4))
    gp, gpp, n1, x = (sent.at[i] for i in range(4, 8))

    def piece(ref, rows):
        return ref.at[pl.ds(rows[0], rows[1])]

    e_moves = [Move(piece(E, r), piece(EL, r), True) for r in ROWS]
    h_move = Move(h, zl.at[0], True)
    t_moves = [Move(piece(T, r), piece(TL, r), False) for r in HALVES]
    cv_moves = [Move(piece(CV, r), piece(CVL, r), True) for r in HALVES]
    cg_move, gp_move = Move(cg, zl.at[1], True), Move(gp, zr.at[0], False)
    m1_move, gpp_move = Move(m1, zl.at[2], True), Move(gpp, zr.at[1], False)
    m2_move, n1_move = Move(m2, zl.at[3], True), Move(n1, zr.at[2], False)
    x_move = Move(x, zr.at[3], False)

    loads["do"].wait()
    loads["uo"].wait()
    for i, r in enumerate(ROWS):
        E[pl.ds(*r), :] = mm(do[pl.ds(*r), :], uo[...]).astype(BF16)
        if i == 0:
            pl.semaphore_wait(barrier, has_l.astype(jnp.int32) + has_r.astype(jnp.int32))
        e_moves[i].start()
        if i == 0:
            for move in moves:
                move.blank()
            loads["ro"].wait()
            h[...] = mv(ro[...].T, do[...]).astype(BF16)
            h_move.start()
    loads["lo"].wait()
    C[...] = mm(do[...], lo[...]).astype(BF16)
    loads["de"].wait()
    loads["ue"].wait()
    B[...] = mm(de[...], ue[...]).astype(BF16)
    loads["le"].wait()
    A[...] = mm(de[...], le[...]).astype(BF16)
    loads["re"].wait()
    g = mv(re[...].T, de[...])
    K[...] = mm(B[...], C[...]).astype(BF16)
    J[...] = mm(B[...], E[...]).astype(BF16)
    CA[...] = mm(C[...], A[...]).astype(BF16)
    fsum[0] = A[...].astype(F32) + mm(K[...], A[...])
    fsum[1] = J[...].astype(F32) + mm(K[...], J[...])
    V[...] = fsum[1].astype(BF16)
    fsum[2] = mm(C[...], V[...])
    q = g - mv(h[...], B[...])
    h_move.arrive()
    q = (q - mv(zl[0], A[...])).astype(BF16)
    qk = q.astype(F32) + mv(q, K[...])

    for i, r in enumerate(ROWS):
        e_moves[i].arrive()
        rows = pl.ds(*r)
        EA[rows, :] = mm(EL[rows, :], A[...]).astype(BF16)
        ta = mm(A[:, rows], EA[rows, :])
        if i < len(ROWS) - 1:
            fsum[0] += ta
        else:
            T[...] = (fsum[0] + ta).astype(BF16)
            t_moves[0].start()
        EJ[rows, :] = mm(EL[rows, :], J[...]).astype(BF16)
        cv = mm(CA[:, rows], EJ[rows, :])
        if i < len(ROWS) - 1:
            fsum[2] += cv
        else:
            CV[...] = (fsum[2] + cv).astype(BF16)
            cv_moves[0].start()
    gpf = qk + mv(mv(q, EL[...]).astype(BF16), A[...])
    gp[...] = gpf.astype(BF16)
    gp_move.start()
    cg[...] = mv(gp[...], C[...]).astype(BF16)
    cg_move.start()
    t_moves[1].start()
    cv_moves[1].start()
    V[...] = (fsum[1] + mm(A[...], EJ[...])).astype(BF16)

    gp_move.arrive()
    cg_move.arrive()
    wide[0] = gp[...].astype(F32) + mv(zl[1], T[...]) + mv(zr[0], V[...])
    r, hold = narrow.at[0], narrow.at[1]
    r[...] = wide[0].astype(BF16)
    for i, rows in enumerate(HALVES):
        t_moves[i].arrive()
        WR[pl.ds(*rows), :] = mm(TL[pl.ds(*rows), :], C[...]).astype(BF16)
    hold[...] = mv(r[...], WR[...]).astype(BF16)
    wide[0] += mv(hold[...], V[...])
    for i in range(len(HALVES)):
        cv_moves[i].arrive()
    hold[...] = mv(r[...], CVL[...]).astype(BF16)
    wide[0] += mv(hold[...], T[...])
    gpp[...] = wide[0].astype(BF16)
    gpp_move.start()
    m1[...] = mv(gpp[...], WR[...]).astype(BF16)
    m1_move.start()
    diagonal = lax.broadcasted_iota(jnp.int32, (n, n), 0) == lax.broadcasted_iota(jnp.int32, (n, n), 1)
    S[...] = (
        jnp.where(diagonal, 1.0, 0.0) + mm(T[...], CVL[...]) + mm(V[...], WR[...])
    ).astype(BF16)
    gpp_move.arrive()
    n1[...] = mv(zr[1], V[...]).astype(BF16)
    n1_move.start()
    m1_move.arrive()
    m2[...] = mv(zl[2], WR[...]).astype(BF16)
    m2_move.start()
    n1_move.arrive()
    w = mv(zr[2], V[...])
    m2_move.arrive()
    w = (w + zl[3].astype(F32)).astype(BF16)
    x[...] = (wide[0] + mv(w, S[...])).astype(BF16)
    x_move.start()
    out[0] = x[...].T
    y = h[...].astype(F32) - mv(x[...], C[...])
    x_move.arrive()
    out[1] = (y - mv(zr[3], E[...])).astype(BF16).T
    for move in moves:
        move.drain()


def body(diag_inverse, lower_block, upper_block, right_side):
    rows, n, nrhs = right_side.shape
    groups, slab = lax.axis_size("grp"), lax.axis_size("dev")

    def kernel(*refs):
        sweep(groups, slab, *refs)

    return pl.pallas_call(
        kernel,
        name="sweep",
        out_shape=jax.ShapeDtypeStruct((rows, n, nrhs), BF16),
        in_specs=[pl.BlockSpec(memory_space=pl.ANY)] * 4,
        out_specs=pl.BlockSpec(memory_space=pltpu.VMEM),
        scratch_shapes=[
            pltpu.VMEM((23, n, n), BF16),
            pltpu.VMEM((rows, n, nrhs), BF16),
            pltpu.VMEM((4, nrhs, n), BF16),
            pltpu.VMEM((4, nrhs, n), BF16),
            pltpu.VMEM((3, n, n), F32),
            pltpu.VMEM((8, nrhs, n), BF16),
            pltpu.VMEM((n // 2, n), BF16),
            pltpu.VMEM((2, nrhs, n), BF16),
            pltpu.VMEM((1, nrhs, n), F32),
            pltpu.SemaphoreType.DMA((8,)),
            pltpu.SemaphoreType.DMA((15,)),
            pltpu.SemaphoreType.DMA((15,)),
        ],
        compiler_params=pltpu.CompilerParams(
            collective_id=0, has_side_effects=True, vmem_limit_bytes=62 * 2**20
        ),
    )(diag_inverse, lower_block, upper_block, right_side)


def solution(mesh):
    spec = P(("grp", "dev"), None, None)
    return jax.shard_map(body, mesh=mesh, in_specs=(spec,) * 4, out_specs=spec, check_vma=False)
```

time: 119 us -> 68.2 us (0.57)
  the two profiles are of different devices: /device:TPU:6 before, /device:TPU:3 now
where the time goes in v1:
time: 68.2 us; the launch traced here: 68 us
  Pallas kernels  66.3 us (97%)
  local copies, waits for them, and re-layouts  1.67 us (2%)
    pallas_call x1, Pallas kernels, body(): pl.pallas_call(kernel, name='sweep', out_shape=jax.ShapeDtypeStruct((rows...  66.3 us
    unnamed x1, local copies, waits for them, and re-layouts  1.67 us

profile of v1, /device:TPU:3, one launch (start us, length us, event | category | flops | bytes accessed | tf_op | source)
XLA Modules:
  0.0 68.0 jit_solution(3014527413465385816)
XLA Ops:
  0.0 66.3 %sweep.1 = bf16[2,512,128]{2,1,0:T(8,128)(2,1)} custom-call(bf16[2,512,512]{2,1,0:T(8,128)(2,1)} %refs_0_.1, bf16[2,512,512]{2,1,0:T(8,128)(2,1)} %refs_1_.1, bf16[2,512,512]{2,1,0:T(8,128)(2,1)} %refs_2_.1, bf16[2,512,128]{2,1,0:T(8,128)(2,1)} %refs_3_.1), custom_call_target="tpu_custom_call" | custom-call | tf_op jit(solution)/shard_map/sweep/pallas_call | solution.py:209
  66.4 1.7 %copy.6 = bf16[2,512,128]{2,1,0:T(8,128)(2,1)} copy(bf16[2,512,128]{2,1,0:T(8,128)(2,1)} %sweep.1) | data formatting | bytes 524288

commit v2 on v1

--- a/solution.py
+++ b/solution.py
@@ -7,7 +7,8 @@
 
 F32, BF16 = jnp.float32, jnp.bfloat16
 MESH = pl.DeviceIdType.MESH
-ROWS = ((0, 256), (256, 128), (384, 128))
+ROWS = ((0, 128), (128, 128), (256, 128), (384, 128))
+COLUMNS = ((0, 64), (64, 64))
 HALVES = ((0, 256), (256, 256))
 
 
@@ -39,10 +40,6 @@
     def _():
         pl.semaphore_signal(barrier, 1, device_id=left, device_id_type=MESH)
 
-    @pl.when(has_r)
-    def _():
-        pl.semaphore_signal(barrier, 1, device_id=right_id, device_id_type=MESH)
-
     loads = {}
     order = (
         ("do", diag.at[1], do), ("uo", upper.at[1], uo), ("ro", right.at[1], ro),
@@ -51,7 +48,8 @@
     )
     for i, (name, src, dst) in enumerate(order):
         loads[name] = pltpu.make_async_copy(src, dst, load.at[i])
-        loads[name].start()
+        if i < 2:
+            loads[name].start()
 
     moves = []
 
@@ -93,23 +91,27 @@
     t_moves = [Move(piece(T, r), piece(TL, r), False) for r in HALVES]
     cv_moves = [Move(piece(CV, r), piece(CVL, r), True) for r in HALVES]
     cg_move, gp_move = Move(cg, zl.at[1], True), Move(gp, zr.at[0], False)
-    m1_move, gpp_move = Move(m1, zl.at[2], True), Move(gpp, zr.at[1], False)
-    m2_move, n1_move = Move(m2, zl.at[3], True), Move(n1, zr.at[2], False)
-    x_move = Move(x, zr.at[3], False)
+    m1_moves = [Move(piece(m1, c), piece(zl.at[2], c), True) for c in COLUMNS]
+    gpp_moves = [Move(piece(gpp, c), piece(zr.at[1], c), False) for c in COLUMNS]
+    m2_moves = [Move(piece(m2, c), piece(zl.at[3], c), True) for c in COLUMNS]
+    n1_moves = [Move(piece(n1, c), piece(zr.at[2], c), False) for c in COLUMNS]
+    x_moves = [Move(piece(x, c), piece(zr.at[3], c), False) for c in COLUMNS]
 
     loads["do"].wait()
     loads["uo"].wait()
+    for name, _, _ in order[2:]:
+        loads[name].start()
     for i, r in enumerate(ROWS):
         E[pl.ds(*r), :] = mm(do[pl.ds(*r), :], uo[...]).astype(BF16)
         if i == 0:
-            pl.semaphore_wait(barrier, has_l.astype(jnp.int32) + has_r.astype(jnp.int32))
+            pl.when(has_r)(lambda: pl.semaphore_wait(barrier, 1))
         e_moves[i].start()
         if i == 0:
             for move in moves:
                 move.blank()
-            loads["ro"].wait()
-            h[...] = mv(ro[...].T, do[...]).astype(BF16)
-            h_move.start()
+    loads["ro"].wait()
+    h[...] = mv(ro[...].T, do[...]).astype(BF16)
+    h_move.start()
     loads["lo"].wait()
     C[...] = mm(do[...], lo[...]).astype(BF16)
     loads["de"].wait()
@@ -127,9 +129,7 @@
     V[...] = fsum[1].astype(BF16)
     fsum[2] = mm(C[...], V[...])
     q = g - mv(h[...], B[...])
-    h_move.arrive()
-    q = (q - mv(zl[0], A[...])).astype(BF16)
-    qk = q.astype(F32) + mv(q, K[...])
+    wide[0] = q
 
     for i, r in enumerate(ROWS):
         e_moves[i].arrive()
@@ -148,8 +148,14 @@
         else:
             CV[...] = (fsum[2] + cv).astype(BF16)
             cv_moves[0].start()
-    gpf = qk + mv(mv(q, EL[...]).astype(BF16), A[...])
-    gp[...] = gpf.astype(BF16)
+    r, hold = narrow.at[0], narrow.at[1]
+    h_move.arrive()
+    wide[0] -= mv(zl[0], A[...])
+    r[...] = wide[0].astype(BF16)
+    hold[...] = mv(r[...], EL[...]).astype(BF16)
+    wide[0] = r[...].astype(F32) + mv(r[...], K[...])
+    wide[0] += mv(hold[...], A[...])
+    gp[...] = wide[0].astype(BF16)
     gp_move.start()
     cg[...] = mv(gp[...], C[...]).astype(BF16)
     cg_move.start()
@@ -160,7 +166,6 @@
     gp_move.arrive()
     cg_move.arrive()
     wide[0] = gp[...].astype(F32) + mv(zl[1], T[...]) + mv(zr[0], V[...])
-    r, hold = narrow.at[0], narrow.at[1]
     r[...] = wide[0].astype(BF16)
     for i, rows in enumerate(HALVES):
         t_moves[i].arrive()
@@ -172,29 +177,38 @@
     hold[...] = mv(r[...], CVL[...]).astype(BF16)
     wide[0] += mv(hold[...], T[...])
     gpp[...] = wide[0].astype(BF16)
-    gpp_move.start()
+    gpp_moves[0].start()
     m1[...] = mv(gpp[...], WR[...]).astype(BF16)
-    m1_move.start()
+    m1_moves[0].start()
+    gpp_moves[1].start()
+    m1_moves[1].start()
     diagonal = lax.broadcasted_iota(jnp.int32, (n, n), 0) == lax.broadcasted_iota(jnp.int32, (n, n), 1)
     S[...] = (
         jnp.where(diagonal, 1.0, 0.0) + mm(T[...], CVL[...]) + mm(V[...], WR[...])
     ).astype(BF16)
-    gpp_move.arrive()
-    n1[...] = mv(zr[1], V[...]).astype(BF16)
-    n1_move.start()
-    m1_move.arrive()
-    m2[...] = mv(zl[2], WR[...]).astype(BF16)
-    m2_move.start()
-    n1_move.arrive()
-    w = mv(zr[2], V[...])
-    m2_move.arrive()
-    w = (w + zl[3].astype(F32)).astype(BF16)
-    x[...] = (wide[0] + mv(w, S[...])).astype(BF16)
-    x_move.start()
-    out[0] = x[...].T
-    y = h[...].astype(F32) - mv(x[...], C[...])
-    x_move.arrive()
-    out[1] = (y - mv(zr[3], E[...])).astype(BF16).T
+    for i, c in enumerate(COLUMNS):
+        c = pl.ds(*c)
+        gpp_moves[i].arrive()
+        n1[c, :] = mv(zr[1, c, :], V[...]).astype(BF16)
+        n1_moves[i].start()
+        m1_moves[i].arrive()
+        m2[c, :] = mv(zl[2, c, :], WR[...]).astype(BF16)
+        m2_moves[i].start()
+    for i, c in enumerate(COLUMNS):
+        c = pl.ds(*c)
+        n1_moves[i].arrive()
+        w = mv(zr[2, c, :], V[...])
+        m2_moves[i].arrive()
+        hold[c, :] = (w + zl[3, c, :].astype(F32)).astype(BF16)
+        x[c, :] = (wide[0, c, :] + mv(hold[c, :], S[...])).astype(BF16)
+        x_moves[i].start()
+    out[0] = x[...].astype(F32).T
+    wide[0] = h[...].astype(F32) - mv(x[...], C[...])
+    for i, c in enumerate(COLUMNS):
+        c = pl.ds(*c)
+        x_moves[i].arrive()
+        wide[0, c, :] -= mv(zr[3, c, :], E[...])
+    out[1] = wide[0].T
     for move in moves:
         move.drain()
 
@@ -209,7 +223,7 @@
     return pl.pallas_call(
         kernel,
         name="sweep",
-        out_shape=jax.ShapeDtypeStruct((rows, n, nrhs), BF16),
+        out_shape=jax.ShapeDtypeStruct((rows, n, nrhs), F32),
         in_specs=[pl.BlockSpec(memory_space=pl.ANY)] * 4,
         out_specs=pl.BlockSpec(memory_space=pltpu.VMEM),
         scratch_shapes=[
@@ -223,13 +237,13 @@
             pltpu.VMEM((2, nrhs, n), BF16),
             pltpu.VMEM((1, nrhs, n), F32),
             pltpu.SemaphoreType.DMA((8,)),
-            pltpu.SemaphoreType.DMA((15,)),
-            pltpu.SemaphoreType.DMA((15,)),
+            pltpu.SemaphoreType.DMA((21,)),
+            pltpu.SemaphoreType.DMA((21,)),
         ],
         compiler_params=pltpu.CompilerParams(
             collective_id=0, has_side_effects=True, vmem_limit_bytes=62 * 2**20
         ),
-    )(diag_inverse, lower_block, upper_block, right_side)
+    )(diag_inverse, lower_block, upper_block, right_side).astype(BF16)
 
 
 def solution(mesh):

time: 68.2 us -> 62.6 us (0.918)
  the two profiles are of different devices: /device:TPU:3 before, /device:TPU:5 now
where the time goes in v2:
time: 62.6 us; the launch traced here: 62.4 us
  Pallas kernels  60.6 us (97%)
  other arithmetic  1.78 us (3%)
    pallas_call x1, Pallas kernels, body(): pl.pallas_call(kernel, name='sweep', out_shape=jax.ShapeDtypeStruct((rows...  60.6 us
    convert_element_type x1, other arithmetic, body(): return pl.pallas_call(kernel, name='sweep', out_shape=jax.ShapeDtypeStruc...  1.78 us

profile of v2, /device:TPU:5, one launch (start us, length us, event | category | flops | bytes accessed | tf_op | source)
XLA Modules:
  0.0 62.4 jit_solution(4024255923780401298)
XLA Ops:
  0.0 60.6 %sweep.1 = f32[2,512,128]{2,1,0:T(8,128)} custom-call(bf16[2,512,512]{2,1,0:T(8,128)(2,1)} %refs_0_.1, bf16[2,512,512]{2,1,0:T(8,128)(2,1)} %refs_1_.1, bf16[2,512,512]{2,1,0:T(8,128)(2,1)} %refs_2_.1, bf16[2,512,128]{2,1,0:T(8,128)(2,1)} %refs_3_.1), custom_call_target="tpu_custom_call" | custom-call | tf_op jit(solution)/shard_map/sweep/pallas_call | solution.py:223
  60.6 1.8 %convert_element_type.3 = bf16[2,512,128]{2,1,0:T(8,128)(2,1)} convert(f32[2,512,128]{2,1,0:T(8,128)} %sweep.1) | non-fusion elementwise | flops 131072 | bytes 786432 | tf_op jit(solution)/shard_map/convert_element_type | solution.py:246

commit v3 on v2

--- a/solution.py
+++ b/solution.py
@@ -135,18 +135,19 @@
         e_moves[i].arrive()
         rows = pl.ds(*r)
         EA[rows, :] = mm(EL[rows, :], A[...]).astype(BF16)
-        ta = mm(A[:, rows], EA[rows, :])
         if i < len(ROWS) - 1:
-            fsum[0] += ta
-        else:
-            T[...] = (fsum[0] + ta).astype(BF16)
+            fsum[0] += mm(A[:, rows], EA[rows, :])
+            EJ[rows, :] = mm(EL[rows, :], J[...]).astype(BF16)
+            fsum[2] += mm(CA[:, rows], EJ[rows, :])
+    last = pl.ds(*ROWS[-1])
+    for i, half in enumerate(HALVES):
+        half = pl.ds(*half)
+        T[half, :] = (fsum[0, half, :] + mm(A[half, last], EA[last, :])).astype(BF16)
+        if i == 0:
             t_moves[0].start()
-        EJ[rows, :] = mm(EL[rows, :], J[...]).astype(BF16)
-        cv = mm(CA[:, rows], EJ[rows, :])
-        if i < len(ROWS) - 1:
-            fsum[2] += cv
-        else:
-            CV[...] = (fsum[2] + cv).astype(BF16)
+            EJ[last, :] = mm(EL[last, :], J[...]).astype(BF16)
+        CV[half, :] = (fsum[2, half, :] + mm(CA[half, last], EJ[last, :])).astype(BF16)
+        if i == 0:
             cv_moves[0].start()
     r, hold = narrow.at[0], narrow.at[1]
     h_move.arrive()
@@ -202,29 +203,51 @@
         hold[c, :] = (w + zl[3, c, :].astype(F32)).astype(BF16)
         x[c, :] = (wide[0, c, :] + mv(hold[c, :], S[...])).astype(BF16)
         x_moves[i].start()
-    out[0] = x[...].astype(F32).T
+    out[0] = x[...].T
     wide[0] = h[...].astype(F32) - mv(x[...], C[...])
     for i, c in enumerate(COLUMNS):
         c = pl.ds(*c)
         x_moves[i].arrive()
         wide[0, c, :] -= mv(zr[3, c, :], E[...])
-    out[1] = wide[0].T
+    out[1] = wide[0].astype(BF16).T
     for move in moves:
         move.drain()
+
+
+def store(swept):
+    def kernel(source, target, sem):
+        copy = pltpu.make_async_copy(source, target, sem)
+        copy.start()
+        copy.wait()
+
+    return pl.pallas_call(
+        kernel,
+        name="store",
+        out_shape=jax.ShapeDtypeStruct(swept.shape, swept.dtype),
+        in_specs=[pl.BlockSpec(memory_space=pltpu.VMEM)],
+        out_specs=pl.BlockSpec(memory_space=pltpu.HBM),
+        scratch_shapes=[pltpu.SemaphoreType.DMA],
+        compiler_params=pltpu.CompilerParams(vmem_limit_bytes=16 * 2**20),
+    )(swept)
 
 
 def body(diag_inverse, lower_block, upper_block, right_side):
     rows, n, nrhs = right_side.shape
     groups, slab = lax.axis_size("grp"), lax.axis_size("dev")
 
+    args = [
+        pltpu.with_memory_space_constraint(a, pltpu.HBM)
+        for a in (diag_inverse, lower_block, upper_block, right_side)
+    ]
+
     def kernel(*refs):
         sweep(groups, slab, *refs)
 
-    return pl.pallas_call(
+    swept = pl.pallas_call(
         kernel,
         name="sweep",
-        out_shape=jax.ShapeDtypeStruct((rows, n, nrhs), F32),
-        in_specs=[pl.BlockSpec(memory_space=pl.ANY)] * 4,
+        out_shape=jax.ShapeDtypeStruct((rows, n, nrhs), BF16),
+        in_specs=[pl.BlockSpec(memory_space=pltpu.HBM)] * 4,
         out_specs=pl.BlockSpec(memory_space=pltpu.VMEM),
         scratch_shapes=[
             pltpu.VMEM((23, n, n), BF16),
@@ -241,9 +264,10 @@
             pltpu.SemaphoreType.DMA((21,)),
         ],
         compiler_params=pltpu.CompilerParams(
-            collective_id=0, has_side_effects=True, vmem_limit_bytes=62 * 2**20
+            collective_id=0, has_side_effects=True, vmem_limit_bytes=40000000
         ),
-    )(diag_inverse, lower_block, upper_block, right_side).astype(BF16)
+    )(*args)
+    return store(swept)
 
 
 def solution(mesh):

time: 62.6 us -> 60.6 us (0.968)
  other arithmetic: 1.78 us -> 0 us
    convert_element_type x1 -> x0, other arithmetic: 1.78 us -> none  [body(): return pl.pallas_call(kernel, name='sweep', out_shape=jax.ShapeDtypeStruc...]
    pallas_call x1, Pallas kernels: 60.6 us -> 59.7 us  [body(): pl.pallas_call(kernel, name='sweep', out_shape=jax.ShapeDtypeStruct((rows...]
    pallas_call x0 -> x1, Pallas kernels: none -> 0.71 us  [store(): pl.pallas_call(kernel, name='store', out_shape=jax.ShapeDtypeStruct(swept...]
where the time goes in v3:
time: 60.6 us; the launch traced here: 60.4 us
  Pallas kernels  60.4 us (100%)
    pallas_call x1, Pallas kernels, body(): pl.pallas_call(kernel, name='sweep', out_shape=jax.ShapeDtypeStruct((rows...  59.7 us

profile of v3, /device:TPU:5, one launch (start us, length us, event | category | flops | bytes accessed | tf_op | source)
XLA Modules:
  0.0 60.4 jit_solution(2694083393728750984)
XLA Ops:
  0.0 59.7 %sweep.1.source = bf16[2,512,128]{2,1,0:T(8,128)(2,1)S(1)} custom-call(bf16[2,512,512]{2,1,0:T(8,128)(2,1)} %refs_0_.1, bf16[2,512,512]{2,1,0:T(8,128)(2,1)} %refs_1_.1, bf16[2,512,512]{2,1,0:T(8,128)(2,1)} %refs_2_.1, bf16[2,512,128]{2,1,0:T(8,128)(2,1)} %refs_3_.1), custom_call_target="tpu_custom_call" | custom-call | tf_op jit(solution)/shard_map/sweep/pallas_call | solution.py:246
  59.7 0.7 %store.1 = bf16[2,512,128]{2,1,0:T(8,128)(2,1)} custom-call(bf16[2,512,128]{2,1,0:T(8,128)(2,1)S(1)} %sweep.1.source), custom_call_target="tpu_custom_call" | custom-call | tf_op jit(solution)/shard_map/store/pallas_call | solution.py:223

commit v4 on v3

--- a/solution.py
+++ b/solution.py
@@ -8,7 +8,7 @@
 F32, BF16 = jnp.float32, jnp.bfloat16
 MESH = pl.DeviceIdType.MESH
 ROWS = ((0, 128), (128, 128), (256, 128), (384, 128))
-COLUMNS = ((0, 64), (64, 64))
+COLUMNS = ((0, 32), (32, 32), (64, 32), (96, 32))
 HALVES = ((0, 256), (256, 256))
 
 
@@ -20,7 +20,7 @@
     return lax.dot_general(rows, matrix, (((1,), (1,)), ((), ())), preferred_element_type=F32)
 
 
-def sweep(groups, slab, diag, lower, upper, right, out, bufs, rhs, zl, zr, fsum, sent, zero, narrow, wide, load, tx, rx):
+def sweep(groups, slab, diag, lower, upper, right, out, bufs, rhs, zl, zr, fsum, sent, zero, narrow, wide, greet, load, tx, rx):
     n = diag.shape[1]
     total = groups * slab
     me = lax.axis_index("grp") * slab + lax.axis_index("dev")
@@ -29,8 +29,8 @@
     left = (at_l // slab, lax.rem(at_l, slab))
     right_id = (at_r // slab, lax.rem(at_r, slab))
     (do, uo, lo, de, le, ue) = (bufs.at[i] for i in range(6))
-    (A, B, C, E, J, K, CA, T, V, CV, EL, TL, CVL, WR, S, EA, EJ) = (
-        bufs.at[i] for i in range(6, 23)
+    (A, B, C, E, J, K, CA, T, V, CV, EL, TL, CVL, WR, S, EA, EJ, T0, AL, XL) = (
+        bufs.at[i] for i in range(6, 26)
     )
     ro, re = rhs.at[0], rhs.at[1]
 
@@ -42,9 +42,9 @@
 
     loads = {}
     order = (
-        ("do", diag.at[1], do), ("uo", upper.at[1], uo), ("ro", right.at[1], ro),
-        ("lo", lower.at[1], lo), ("de", diag.at[0], de), ("ue", upper.at[0], ue),
-        ("le", lower.at[0], le), ("re", right.at[0], re),
+        ("do", diag.at[1], do), ("uo", upper.at[1], uo), ("de", diag.at[0], de),
+        ("le", lower.at[0], le), ("ro", right.at[1], ro), ("lo", lower.at[1], lo),
+        ("ue", upper.at[0], ue), ("re", right.at[0], re),
     )
     for i, (name, src, dst) in enumerate(order):
         loads[name] = pltpu.make_async_copy(src, dst, load.at[i])
@@ -88,7 +88,8 @@
 
     e_moves = [Move(piece(E, r), piece(EL, r), True) for r in ROWS]
     h_move = Move(h, zl.at[0], True)
-    t_moves = [Move(piece(T, r), piece(TL, r), False) for r in HALVES]
+    a_moves = [Move(piece(A, r), piece(AL, r), False) for r in HALVES]
+    t_moves = [Move(piece(T0, r), piece(TL, r), False) for r in HALVES]
     cv_moves = [Move(piece(CV, r), piece(CVL, r), True) for r in HALVES]
     cg_move, gp_move = Move(cg, zl.at[1], True), Move(gp, zr.at[0], False)
     m1_moves = [Move(piece(m1, c), piece(zl.at[2], c), True) for c in COLUMNS]
@@ -104,51 +105,59 @@
     for i, r in enumerate(ROWS):
         E[pl.ds(*r), :] = mm(do[pl.ds(*r), :], uo[...]).astype(BF16)
         if i == 0:
-            pl.when(has_r)(lambda: pl.semaphore_wait(barrier, 1))
+
+            @pl.when(has_r)
+            def _():
+                pl.semaphore_wait(barrier, 1)
+                pl.semaphore_signal(greet, 1, device_id=right_id, device_id_type=MESH)
+
         e_moves[i].start()
         if i == 0:
             for move in moves:
                 move.blank()
+    loads["de"].wait()
+    loads["le"].wait()
+    A[...] = mm(de[...], le[...]).astype(BF16)
+    pl.when(has_l)(lambda: pl.semaphore_wait(greet, 1))
+    for move in a_moves:
+        move.start()
     loads["ro"].wait()
     h[...] = mv(ro[...].T, do[...]).astype(BF16)
     h_move.start()
     loads["lo"].wait()
     C[...] = mm(do[...], lo[...]).astype(BF16)
-    loads["de"].wait()
     loads["ue"].wait()
     B[...] = mm(de[...], ue[...]).astype(BF16)
-    loads["le"].wait()
-    A[...] = mm(de[...], le[...]).astype(BF16)
+    K[...] = mm(B[...], C[...]).astype(BF16)
+    fsum[0] = A[...].astype(F32) + mm(K[...], A[...])
+    T0[...] = fsum[0].astype(BF16)
+    for move in t_moves:
+        move.start()
     loads["re"].wait()
-    g = mv(re[...].T, de[...])
-    K[...] = mm(B[...], C[...]).astype(BF16)
     J[...] = mm(B[...], E[...]).astype(BF16)
     CA[...] = mm(C[...], A[...]).astype(BF16)
-    fsum[0] = A[...].astype(F32) + mm(K[...], A[...])
     fsum[1] = J[...].astype(F32) + mm(K[...], J[...])
     V[...] = fsum[1].astype(BF16)
     fsum[2] = mm(C[...], V[...])
-    q = g - mv(h[...], B[...])
-    wide[0] = q
-
-    for i, r in enumerate(ROWS):
+    wide[0] = mv(re[...].T, de[...])
+    wide[0] -= mv(h[...], B[...])
+
+    for i, rows in enumerate(ROWS):
+        rows = pl.ds(*rows)
         e_moves[i].arrive()
-        rows = pl.ds(*r)
-        EA[rows, :] = mm(EL[rows, :], A[...]).astype(BF16)
+        EJ[rows, :] = mm(EL[rows, :], J[...]).astype(BF16)
         if i < len(ROWS) - 1:
+            fsum[2] += mm(CA[:, rows], EJ[rows, :])
+            EA[rows, :] = mm(EL[rows, :], A[...]).astype(BF16)
             fsum[0] += mm(A[:, rows], EA[rows, :])
-            EJ[rows, :] = mm(EL[rows, :], J[...]).astype(BF16)
-            fsum[2] += mm(CA[:, rows], EJ[rows, :])
     last = pl.ds(*ROWS[-1])
     for i, half in enumerate(HALVES):
         half = pl.ds(*half)
-        T[half, :] = (fsum[0, half, :] + mm(A[half, last], EA[last, :])).astype(BF16)
-        if i == 0:
-            t_moves[0].start()
-            EJ[last, :] = mm(EL[last, :], J[...]).astype(BF16)
         CV[half, :] = (fsum[2, half, :] + mm(CA[half, last], EJ[last, :])).astype(BF16)
         if i == 0:
             cv_moves[0].start()
+    EA[last, :] = mm(EL[last, :], A[...]).astype(BF16)
+    T[...] = (fsum[0] + mm(A[:, last], EA[last, :])).astype(BF16)
     r, hold = narrow.at[0], narrow.at[1]
     h_move.arrive()
     wide[0] -= mv(zl[0], A[...])
@@ -160,17 +169,23 @@
     gp_move.start()
     cg[...] = mv(gp[...], C[...]).astype(BF16)
     cg_move.start()
-    t_moves[1].start()
     cv_moves[1].start()
     V[...] = (fsum[1] + mm(A[...], EJ[...])).astype(BF16)
+
+    for move in a_moves:
+        move.arrive()
+    XL[...] = mm(E[...], AL[...]).astype(BF16)
+    fsum[0] = mm(AL[...], XL[...])
+    for i, half in enumerate(HALVES):
+        half = pl.ds(*half)
+        t_moves[i].arrive()
+        XL[half, :] = (fsum[0, half, :] + TL[half, :].astype(F32)).astype(BF16)
+        WR[half, :] = mm(XL[half, :], C[...]).astype(BF16)
 
     gp_move.arrive()
     cg_move.arrive()
     wide[0] = gp[...].astype(F32) + mv(zl[1], T[...]) + mv(zr[0], V[...])
     r[...] = wide[0].astype(BF16)
-    for i, rows in enumerate(HALVES):
-        t_moves[i].arrive()
-        WR[pl.ds(*rows), :] = mm(TL[pl.ds(*rows), :], C[...]).astype(BF16)
     hold[...] = mv(r[...], WR[...]).astype(BF16)
     wide[0] += mv(hold[...], V[...])
     for i in range(len(HALVES)):
@@ -181,20 +196,48 @@
     gpp_moves[0].start()
     m1[...] = mv(gpp[...], WR[...]).astype(BF16)
     m1_moves[0].start()
-    gpp_moves[1].start()
-    m1_moves[1].start()
+    for i in range(1, len(COLUMNS)):
+        gpp_moves[i].start()
+        m1_moves[i].start()
     diagonal = lax.broadcasted_iota(jnp.int32, (n, n), 0) == lax.broadcasted_iota(jnp.int32, (n, n), 1)
     S[...] = (
         jnp.where(diagonal, 1.0, 0.0) + mm(T[...], CVL[...]) + mm(V[...], WR[...])
     ).astype(BF16)
-    for i, c in enumerate(COLUMNS):
-        c = pl.ds(*c)
+    def leftward(i):
+        c = pl.ds(*COLUMNS[i])
         gpp_moves[i].arrive()
         n1[c, :] = mv(zr[1, c, :], V[...]).astype(BF16)
         n1_moves[i].start()
+
+    def rightward(i):
+        c = pl.ds(*COLUMNS[i])
         m1_moves[i].arrive()
         m2[c, :] = mv(zl[2, c, :], WR[...]).astype(BF16)
         m2_moves[i].start()
+
+    pieces = range(len(COLUMNS))
+    spot = lax.rem(me, 8)
+
+    @pl.when(spot == 7)
+    def _():
+        for i in pieces:
+            rightward(i)
+        for i in pieces:
+            leftward(i)
+
+    @pl.when(spot == 0)
+    def _():
+        for i in pieces:
+            leftward(i)
+        for i in pieces:
+            rightward(i)
+
+    @pl.when(jnp.logical_and(spot > 0, spot < 7))
+    def _():
+        for i in pieces:
+            leftward(i)
+            rightward(i)
+
     for i, c in enumerate(COLUMNS):
         c = pl.ds(*c)
         n1_moves[i].arrive()
@@ -250,7 +293,7 @@
         in_specs=[pl.BlockSpec(memory_space=pltpu.HBM)] * 4,
         out_specs=pl.BlockSpec(memory_space=pltpu.VMEM),
         scratch_shapes=[
-            pltpu.VMEM((23, n, n), BF16),
+            pltpu.VMEM((26, n, n), BF16),
             pltpu.VMEM((rows, n, nrhs), BF16),
             pltpu.VMEM((4, nrhs, n), BF16),
             pltpu.VMEM((4, nrhs, n), BF16),
@@ -259,9 +302,10 @@
             pltpu.VMEM((n // 2, n), BF16),
             pltpu.VMEM((2, nrhs, n), BF16),
             pltpu.VMEM((1, nrhs, n), F32),
+            pltpu.SemaphoreType.REGULAR,
             pltpu.SemaphoreType.DMA((8,)),
-            pltpu.SemaphoreType.DMA((21,)),
-            pltpu.SemaphoreType.DMA((21,)),
+            pltpu.SemaphoreType.DMA((33,)),
+            pltpu.SemaphoreType.DMA((33,)),
         ],
         compiler_params=pltpu.CompilerParams(
             collective_id=0, has_side_effects=True, vmem_limit_bytes=40000000

time: 60.6 us -> 60.4 us (level)
  the two profiles are of different devices: /device:TPU:5 before, /device:TPU:6 now
where the time goes in v4:
time: 60.4 us; the launch traced here: 60.3 us
  Pallas kernels  60.2 us (100%)
    pallas_call x1, Pallas kernels, body(): pl.pallas_call(kernel, name='sweep', out_shape=jax.ShapeDtypeStruct((rows...  59.5 us

profile of v4, /device:TPU:6, one launch (start us, length us, event | category | flops | bytes accessed | tf_op | source)
XLA Modules:
  0.0 60.3 jit_solution(1923470833612222180)
XLA Ops:
  0.0 59.5 %sweep.1.source = bf16[2,512,128]{2,1,0:T(8,128)(2,1)S(1)} custom-call(bf16[2,512,512]{2,1,0:T(8,128)(2,1)} %refs_0_.1, bf16[2,512,512]{2,1,0:T(8,128)(2,1)} %refs_1_.1, bf16[2,512,512]{2,1,0:T(8,128)(2,1)} %refs_2_.1, bf16[2,512,128]{2,1,0:T(8,128)(2,1)} %refs_3_.1), custom_call_target="tpu_custom_call" | custom-call | tf_op jit(solution)/shard_map/sweep/pallas_call | solution.py:289
  59.5 0.7 %store.1 = bf16[2,512,128]{2,1,0:T(8,128)(2,1)} custom-call(bf16[2,512,128]{2,1,0:T(8,128)(2,1)S(1)} %sweep.1.source), custom_call_target="tpu_custom_call" | custom-call | tf_op jit(solution)/shard_map/store/pallas_call | solution.py:266

commit v5 on v4

--- a/solution.py
+++ b/solution.py
@@ -154,8 +154,7 @@
     for i, half in enumerate(HALVES):
         half = pl.ds(*half)
         CV[half, :] = (fsum[2, half, :] + mm(CA[half, last], EJ[last, :])).astype(BF16)
-        if i == 0:
-            cv_moves[0].start()
+        cv_moves[i].start()
     EA[last, :] = mm(EL[last, :], A[...]).astype(BF16)
     T[...] = (fsum[0] + mm(A[:, last], EA[last, :])).astype(BF16)
     r, hold = narrow.at[0], narrow.at[1]
@@ -169,7 +168,6 @@
     gp_move.start()
     cg[...] = mv(gp[...], C[...]).astype(BF16)
     cg_move.start()
-    cv_moves[1].start()
     V[...] = (fsum[1] + mm(A[...], EJ[...])).astype(BF16)
 
     for move in a_moves:
@@ -182,16 +180,16 @@
         XL[half, :] = (fsum[0, half, :] + TL[half, :].astype(F32)).astype(BF16)
         WR[half, :] = mm(XL[half, :], C[...]).astype(BF16)
 
+    for move in cv_moves:
+        move.arrive()
+    diagonal = lax.broadcasted_iota(jnp.int32, (n, n), 0) == lax.broadcasted_iota(jnp.int32, (n, n), 1)
+    fsum[0] = jnp.where(diagonal, 1.0, 0.0) + mm(V[...], WR[...])
+    S[...] = (fsum[0] + mm(T[...], CVL[...])).astype(BF16)
     gp_move.arrive()
     cg_move.arrive()
     wide[0] = gp[...].astype(F32) + mv(zl[1], T[...]) + mv(zr[0], V[...])
     r[...] = wide[0].astype(BF16)
-    hold[...] = mv(r[...], WR[...]).astype(BF16)
-    wide[0] += mv(hold[...], V[...])
-    for i in range(len(HALVES)):
-        cv_moves[i].arrive()
-    hold[...] = mv(r[...], CVL[...]).astype(BF16)
-    wide[0] += mv(hold[...], T[...])
+    wide[0] = mv(r[...], S[...])
     gpp[...] = wide[0].astype(BF16)
     gpp_moves[0].start()
     m1[...] = mv(gpp[...], WR[...]).astype(BF16)
@@ -199,10 +197,6 @@
     for i in range(1, len(COLUMNS)):
         gpp_moves[i].start()
         m1_moves[i].start()
-    diagonal = lax.broadcasted_iota(jnp.int32, (n, n), 0) == lax.broadcasted_iota(jnp.int32, (n, n), 1)
-    S[...] = (
-        jnp.where(diagonal, 1.0, 0.0) + mm(T[...], CVL[...]) + mm(V[...], WR[...])
-    ).astype(BF16)
     def leftward(i):
         c = pl.ds(*COLUMNS[i])
         gpp_moves[i].arrive()

time: 60.4 us -> 59.8 us (0.990)
    pallas_call x1, Pallas kernels: 59.5 us -> 58.9 us  [body(): pl.pallas_call(kernel, name='sweep', out_shape=jax.ShapeDtypeStruct((rows...]
where the time goes in v5:
time: 59.8 us; the launch traced here: 59.7 us
  Pallas kernels  59.6 us (100%)
    pallas_call x1, Pallas kernels, body(): pl.pallas_call(kernel, name='sweep', out_shape=jax.ShapeDtypeStruct((rows...  58.9 us

profile of v5, /device:TPU:6, one launch (start us, length us, event | category | flops | bytes accessed | tf_op | source)
XLA Modules:
  0.0 59.7 jit_solution(14805314434091491799)
XLA Ops:
  0.0 58.9 %sweep.1.source = bf16[2,512,128]{2,1,0:T(8,128)(2,1)S(1)} custom-call(bf16[2,512,512]{2,1,0:T(8,128)(2,1)} %refs_0_.1, bf16[2,512,512]{2,1,0:T(8,128)(2,1)} %refs_1_.1, bf16[2,512,512]{2,1,0:T(8,128)(2,1)} %refs_2_.1, bf16[2,512,128]{2,1,0:T(8,128)(2,1)} %refs_3_.1), custom_call_target="tpu_custom_call" | custom-call | tf_op jit(solution)/shard_map/sweep/pallas_call | solution.py:283
  58.9 0.7 %store.1 = bf16[2,512,128]{2,1,0:T(8,128)(2,1)} custom-call(bf16[2,512,128]{2,1,0:T(8,128)(2,1)S(1)} %sweep.1.source), custom_call_target="tpu_custom_call" | custom-call | tf_op jit(solution)/shard_map/store/pallas_call | solution.py:260
